TPU v7x, 32 devices: a whole 2x2x4 slice. The times are simulated.
32 devices in a mesh: row: 8 (over y, x, core), col: 4 (over z).
Axes of the slice: x: 2, y: 2, z: 4, core: 2. Of those that a mesh axis runs over, the one named last changes fastest.
Arguments:
- features: bfloat16 [512, 128, 128], P('row', 'col'), may hold values from -6 to 6
- cotangent: bfloat16 [512, 128, 128], P('row', 'col'), may hold values from -6 to 6
- kernels: bfloat16 [2, 9, 128, 128], replicated, may hold values from -0.1875 to 0.1875
- momentum: float32 [2, 147456], replicated, may hold values from -6 to 6
- mlp_in_weight: float32 [32, 3], replicated, may hold values from -3.5 to 3.5
- mlp_in_bias: float32 [32], replicated, may hold values from -3 to 3
- mlp_out_weight: float32 [2, 32], replicated, may hold values from -1 to 1
- mlp_out_bias: float32 [2], replicated, may hold values from -3 to 3
Outputs:
- update: float32 [2, 147456], replicated
- momentum_out: float32 [2, 147456], replicated
All inputs are finite; a program needn't handle non-finite values.
Results may differ from a plain program's by a relative error of at most 0.0014.
Values may be sent and summed in bfloat16 or wider, within the bound.
A program may use at most 64 MiB of HBM per device.

v0:
```python
import math
import jax
import jax.numpy as jnp
from jax import lax
from jax.sharding import PartitionSpec as P


def padded_2(cells, sides, width):
    for axis, dim in sides:
        count = lax.axis_size(axis)
        head = lax.slice_in_dim(cells, 0, width, axis=dim)
        tail = lax.slice_in_dim(cells, cells.shape[dim] - width, cells.shape[dim], axis=dim)
        cells = jnp.concatenate(
            [
                lax.ppermute(tail, axis, [(i, (i + 1) % count) for i in range(count)]),
                cells,
                lax.ppermute(head, axis, [((i + 1) % count, i) for i in range(count)]),
            ],
            axis=dim,
        )
    return cells


def convolve(padded, kernel, tile_rows, tile_cols):
    channels = padded.shape[-1]
    summed = jnp.zeros((tile_rows * tile_cols, kernel.shape[-1]), jnp.float32)
    for tap_row in range(3):
        for tap_col in range(3):
            window = padded[tap_row : tap_row + tile_rows, tap_col : tap_col + tile_cols].reshape(
                tile_rows * tile_cols, channels
            )
            summed = summed + jnp.dot(
                window, kernel[3 * tap_row + tap_col], preferred_element_type=jnp.float32
            )
    return summed.reshape(tile_rows, tile_cols, -1)


def kernel_grad(padded, cotangent, tile_rows, tile_cols):
    channels = padded.shape[-1]
    flat_cot = cotangent.reshape(tile_rows * tile_cols, -1)
    taps = []
    for tap_row in range(3):
        for tap_col in range(3):
            window = padded[tap_row : tap_row + tile_rows, tap_col : tap_col + tile_cols].reshape(
                tile_rows * tile_cols, channels
            )
            taps.append(
                lax.dot_general(
                    window, flat_cot, (((0,), (0,)), ((), ())), preferred_element_type=jnp.float32
                )
            )
    return jnp.stack(taps)


def transpose_conv(cot_pad, kernel, tile_rows, tile_cols):
    channels = cot_pad.shape[-1]
    summed = jnp.zeros((tile_rows * tile_cols, kernel.shape[-2]), jnp.float32)
    for tap_row in range(3):
        for tap_col in range(3):
            window = cot_pad[
                2 - tap_row : 2 - tap_row + tile_rows, 2 - tap_col : 2 - tap_col + tile_cols
            ].reshape(tile_rows * tile_cols, channels)
            summed = summed + lax.dot_general(
                window,
                kernel[3 * tap_row + tap_col],
                (((1,), (1,)), ((), ())),
                preferred_element_type=jnp.float32,
            )
    return summed.reshape(tile_rows, tile_cols, -1)


def learned_step(grads, squares, momentum, weights, w_in, b_in, w_out, b_out, gain, count):
    norm_scale = 1.0 / jnp.sqrt(squares / count + 1e-06)
    g_hat = grads * norm_scale[:, None]
    momentum_new = 0.9 * momentum + 0.1 * g_hat
    scaled = weights.astype(jnp.float32) * gain
    pre_units = (
        w_in[:, 0][:, None, None] * g_hat[None] + w_in[:, 1][:, None, None] * momentum_new[None]
    )
    pre_units = pre_units + w_in[:, 2][:, None, None] * scaled[None] + b_in[:, None, None]
    units = jax.nn.silu(pre_units)
    mlp_result = (
        jnp.einsum("kh,hlp->klp", w_out, units, precision=lax.Precision.HIGHEST)
        + b_out[:, None, None]
    )
    update = mlp_result[0] * jnp.exp(jnp.tanh(mlp_result[1]))
    return (update, momentum_new)


def on_device(
    features, cotangent, kernels, momentum, mlp_in_weight, mlp_in_bias, mlp_out_weight, mlp_out_bias
):
    tile_rows, tile_cols, channels = features.shape
    param_count = 9 * channels * channels
    image_pad = padded_2(features, (("row", 0), ("col", 1)), 1)
    pre_act = convolve(image_pad, kernels[0], tile_rows, tile_cols)
    hidden = jax.nn.silu(pre_act).astype(jnp.bfloat16)
    hidden_pad = padded_2(hidden, (("row", 0), ("col", 1)), 1)
    cot_pad = padded_2(cotangent, (("row", 0), ("col", 1)), 1)
    grad_two = kernel_grad(hidden_pad, cotangent, tile_rows, tile_cols)
    back_grad = transpose_conv(cot_pad, kernels[1], tile_rows, tile_cols)
    sigma_val = jax.nn.sigmoid(pre_act)
    pre_grad = (back_grad * sigma_val * (1.0 + pre_act * (1.0 - sigma_val))).astype(jnp.bfloat16)
    grad_one = kernel_grad(image_pad, pre_grad, tile_rows, tile_cols)
    local_grads = jnp.stack([grad_one.reshape(-1), grad_two.reshape(-1)])
    weights = kernels.reshape(2, param_count)
    gain = math.sqrt(9.0 * channels)
    grads = lax.psum(local_grads, ("row", "col"))
    squares = jnp.sum(grads * grads, axis=1)
    update, momentum_out = learned_step(
        grads,
        squares,
        momentum,
        weights,
        mlp_in_weight,
        mlp_in_bias,
        mlp_out_weight,
        mlp_out_bias,
        gain,
        float(param_count),
    )
    return (update, momentum_out)


def solution(mesh):
    placed = (P("row", "col", None), P("row", "col", None), P(), P(), P(), P(), P(), P())
    return jax.shard_map(
        on_device, mesh=mesh, in_specs=placed, out_specs=(P(), P()), check_vma=False
    )
```

profile of v0, /device:TPU:0, one launch (start us, length us, event | category | flops | bytes accessed | tf_op | source)
XLA Modules:
  0.0 238.4 jit_solution(3576847353787842551)
XLA Ops:
  7.2 1.3 copy.30
  8.6 0.5 collective-permute-start
  9.1 2.9 %collective-permute-start.1 = (bf16[1,32,128]{2,0,1:T(2,128)(2,1)S(1)}, bf16[1,32,128]{2,0,1:T(2,128)(2,1)S(1)}, u32[]{:S(2)}, u32[]{:S(2)}) collective-permute-start(bf16[1,32,128]{2,0,1:T(2,128)(2,1)S(1)} %get-tuple-element.41), channel_id=1, source_target_pairs={{4,0},{8,4},{12,8},{16,12},{20,16},{24,20},{28,24},{0,28},{5,1},{9... | collective-permute-start | bytes 24584 | tf_op jit(solution)/shard_map/ppermute | solution.py:17
  12.1 0.7 fusion.119
  12.8 2.6 %collective-permute-start.4 = (bf16[1,32,128]{2,1,0:T(8,128)(2,1)S(1)}, bf16[1,32,128]{2,1,0:T(8,128)(2,1)S(1)}, u32[]{:S(2)}, u32[]{:S(2)}) collective-permute-start(bf16[1,32,128]{2,1,0:T(8,128)(2,1)S(1)} %get-tuple-element.34), channel_id=1, source_target_pairs={{4,0},{8,4},{12,8},{16,12},{20,16},{24,20},{28,24},{0,28},{5,1},{9... | collective-permute-start | bytes 24584 | tf_op jit(solution)/shard_map/ppermute | solution.py:17
  15.5 2.3 collective-permute-start.2
  17.8 2.1 collective-permute-start.7
  20.8 0.4 pad_maximum_fusion.7
  21.2 0.3 copy.35
  21.5 0.3 copy.41
  21.9 2.0 collective-permute-start.5
  23.9 0.5 collective-permute-start.6
  24.4 0.3 pad_maximum_fusion.1
  24.8 0.6 fusion.116
  25.4 0.3 copy.33
  26.0 0.3 copy.36
  26.4 0.3 copy.37
  27.8 2.3 collective-permute-done.6
  30.1 0.7 pad_maximum_fusion.11
  32.0 0.7 copy-done.4
  35.7 0.4 fusion.21
  36.0 1.4 fusion.43
  38.5 0.3 fusion.38
  38.8 0.4 fusion.37
  39.2 0.3 fusion.36
  39.6 0.3 fusion.35
  40.1 2.6 %collective-permute-start.9 = (bf16[1,32,128]{2,0,1:T(2,128)(2,1)S(1)}, bf16[1,32,128]{2,0,1:T(2,128)(2,1)S(1)}, u32[]{:S(2)}, u32[]{:S(2)}) collective-permute-start(bf16[1,32,128]{2,0,1:T(2,128)(2,1)S(1)} %get-tuple-element.37), channel_id=1, source_target_pairs={{4,0},{8,4},{12,8},{16,12},{20,16},{24,20},{28,24},{0,28},{5,1},{9... | collective-permute-start | bytes 24584 | tf_op jit(solution)/shard_map/ppermute | solution.py:17
  43.0 1.2 collective-permute-done.8
  44.3 4.0 %collective-permute-start.11 = (bf16[66,1,128]{2,0,1:T(8,128)(2,1)S(1)}, bf16[66,1,128]{2,0,1:T(8,128)(2,1)S(1)}, u32[]{:S(2)}, u32[]{:S(2)}) collective-permute-start(bf16[66,1,128]{2,0,1:T(8,128)(2,1)S(1)} %get-tuple-element.20), channel_id=1, source_target_pairs={{1,0},{2,1},{3,2},{0,3},{5,4},{6,5},{7,6},{4,7},{9,8},{10,9},{11,1... | collective-permute-start | bytes 50696 | tf_op jit(solution)/shard_map/ppermute | solution.py:17
  48.6 1.2 collective-permute-done.10
  49.8 0.4 pad_maximum_fusion.2
  50.2 0.4 fusion.32
  50.6 0.5 fusion.31
  51.1 0.4 fusion.30
  51.4 0.4 fusion.29
  51.9 0.4 fusion.28
  52.3 0.4 fusion.27
  52.7 0.4 fusion.26
  53.2 0.5 fusion.25
  53.7 0.4 fusion.24
  54.1 1.9 pad_maximum_fusion
  56.2 4.3 %copy.91 = f32[1,2,1152,128]{3,1,2,0:T(2,128)S(1)} copy(f32[1,2,1152,128]{3,2,1,0:T(8,128)S(1)} %bitcast.218) | data formatting | bytes 2359296
  60.5 127.9 %all-reduce.2.cloned.1.call-done = f32[2,147456]{1,0:T(2,128)} async-done(((f32[2,147456]{1,0:T(2,128)}), f32[2,147456]{1,0:T(2,128)}) %all-reduce.2.cloned.1.call-update) | async-done | bytes 1179664 | tf_op jit(solution)/shard_map/psum | solution.py:108
  188.4 2.5 %multiply_reduce_fusion = f32[2]{0:T(128)S(1)} fusion(f32[2,147456]{1,0:T(2,128)} %all-reduce.2.cloned.1.call-done), kind=kLoop, calls=%fused_computation.45 | loop fusion | flops 589822 | bytes 1179656 | tf_op jit(solution)/shard_map/reduce_sum | solution.py:109
  191.0 1.3 multiply_add_fusion
  192.4 33.7 %fusion = f32[2,2,147456]{2,0,1:T(2,128)S(1)} fusion(f32[32]{0:T(128)S(1)} %copy-done.8, f32[2,147456]{1,0:T(2,128)S(1)} %bitcast.239, f32[32]{0:T(128)S(1)} %get-tuple-element.43, f32[2,147456]{1,0:T(2,128)S(1)} %get-tuple-element.2, f32[32]{0:T(128)S(1)} %get-tuple-element.44, f32[2,147456]{1,0:T(2,128)S(1)} %get-tuple-element.3, ...), kind=kOutput, calls=%fused_computation.1 | convolution fusion | flops 321454080 | bytes 5899016 | tf_op jit(solution)/shard_map/kh,hlp->klp/dot_general | solution.py:83
  226.1 2.5 %fusion.23 = f32[1,2,147456]{2,0,1:T(1,128)S(1)} fusion(f32[2,2,147456]{2,0,1:T(2,128)S(1)} %fusion), kind=kLoop, calls=%fused_computation.40 | loop fusion | flops 294912 | bytes 3538944 | tf_op jit(solution)/shard_map/mul | solution.py:86
  228.6 2.7 %copy.92 = f32[1,2,147456]{2,1,0:T(2,128)} copy(f32[1,2,147456]{2,0,1:T(1,128)S(1)} %fusion.23) | data formatting | bytes 2359296
  (69 shorter events, 8.4 us)
Async XLA Ops:
  7.2 185.2 %copy-start = (f32[2,32]{1,0:T(2,128)S(1)}, f32[2,32]{1,0:T(2,128)}, u32[]{:S(2)}) copy-start(f32[2,32]{1,0:T(2,128)} %param.14) | copy-start | bytes 772
  7.2 12.7 %copy-start.3 = (bf16[64,32,128]{2,1,0:T(8,128)(2,1)S(1)}, bf16[64,32,128]{2,1,0:T(8,128)(2,1)}, u32[]{:S(2)}) copy-start(bf16[64,32,128]{2,1,0:T(8,128)(2,1)} %param.9) | copy-start | bytes 1572868
  7.2 181.2 %all-reduce.2.cloned.1.call-start = ((), (), s32[]{:S(2)}) async-start(), calls=%async_computation | async-start | bytes 2359296 | tf_op jit(solution)/shard_map/psum | solution.py:108
  8.6 6.8 %collective-permute-start = (bf16[1,32,128]{2,0,1:T(2,128)(2,1)S(1)}, bf16[1,32,128]{2,0,1:T(2,128)(2,1)S(1)}, u32[]{:S(2)}, u32[]{:S(2)}) collective-permute-start(bf16[1,32,128]{2,0,1:T(2,128)(2,1)S(1)} %get-tuple-element.40), channel_id=1, source_target_pairs={{0,4},{4,8},{8,12},{12,16},{16,20},{20,24},{24,28},{28,0},{1,5},{5... | collective-permute-start | bytes 24584 | tf_op jit(solution)/shard_map/ppermute | solution.py:15
  9.1 6.3 %collective-permute-start.1 = (bf16[1,32,128]{2,0,1:T(2,128)(2,1)S(1)}, bf16[1,32,128]{2,0,1:T(2,128)(2,1)S(1)}, u32[]{:S(2)}, u32[]{:S(2)}) collective-permute-start(bf16[1,32,128]{2,0,1:T(2,128)(2,1)S(1)} %get-tuple-element.41), channel_id=1, source_target_pairs={{4,0},{8,4},{12,8},{16,12},{20,16},{24,20},{28,24},{0,28},{5,1},{9... | collective-permute-start | bytes 24584 | tf_op jit(solution)/shard_map/ppermute | solution.py:17
  12.8 7.1 %collective-permute-start.3 = (bf16[1,32,128]{2,1,0:T(8,128)(2,1)S(1)}, bf16[1,32,128]{2,1,0:T(8,128)(2,1)S(1)}, u32[]{:S(2)}, u32[]{:S(2)}) collective-permute-start(bf16[1,32,128]{2,1,0:T(8,128)(2,1)S(1)} %get-tuple-element.35), channel_id=1, source_target_pairs={{0,4},{4,8},{8,12},{12,16},{16,20},{20,24},{24,28},{28,0},{1,5},{5... | collective-permute-start | bytes 24584 | tf_op jit(solution)/shard_map/ppermute | solution.py:15
  12.8 7.1 %collective-permute-start.4 = (bf16[1,32,128]{2,1,0:T(8,128)(2,1)S(1)}, bf16[1,32,128]{2,1,0:T(8,128)(2,1)S(1)}, u32[]{:S(2)}, u32[]{:S(2)}) collective-permute-start(bf16[1,32,128]{2,1,0:T(8,128)(2,1)S(1)} %get-tuple-element.34), channel_id=1, source_target_pairs={{4,0},{8,4},{12,8},{16,12},{20,16},{24,20},{28,24},{0,28},{5,1},{9... | collective-permute-start | bytes 24584 | tf_op jit(solution)/shard_map/ppermute | solution.py:17
  15.4 4.8 %copy-start.2 = (bf16[2,9,128,128]{3,2,1,0:T(8,128)(2,1)S(1)}, bf16[2,9,128,128]{3,2,1,0:T(8,128)(2,1)}, u32[]{:S(2)}) copy-start(bf16[2,9,128,128]{3,2,1,0:T(8,128)(2,1)} %param.10) | copy-start | bytes 1769476
  15.5 9.0 %collective-permute-start.2 = (bf16[66,1,128]{2,0,1:T(8,128)(2,1)S(1)}, bf16[66,1,128]{2,0,1:T(8,128)(2,1)S(1)}, u32[]{:S(2)}, u32[]{:S(2)}) collective-permute-start(bf16[66,1,128]{2,0,1:T(8,128)(2,1)S(1)} %get-tuple-element.25), channel_id=1, source_target_pairs={{0,1},{1,2},{2,3},{3,0},{4,5},{5,6},{6,7},{7,4},{8,9},{9,10},{10,1... | collective-permute-start | bytes 50696 | tf_op jit(solution)/shard_map/ppermute | solution.py:15
  17.8 6.6 %collective-permute-start.7 = (bf16[66,1,128]{2,0,1:T(8,128)(2,1)S(1)}, bf16[66,1,128]{2,0,1:T(8,128)(2,1)S(1)}, u32[]{:S(2)}, u32[]{:S(2)}) collective-permute-start(bf16[66,1,128]{2,0,1:T(8,128)(2,1)S(1)} %get-tuple-element.24), channel_id=1, source_target_pairs={{1,0},{2,1},{3,2},{0,3},{5,4},{6,5},{7,6},{4,7},{9,8},{10,9},{11,1... | collective-permute-start | bytes 50696 | tf_op jit(solution)/shard_map/ppermute | solution.py:17
  21.9 5.9 %collective-permute-start.5 = (bf16[66,1,128]{2,1,0:T(2,128)(2,1)S(1)}, bf16[66,1,128]{2,1,0:T(2,128)(2,1)S(1)}, u32[]{:S(2)}, u32[]{:S(2)}) collective-permute-start(bf16[66,1,128]{2,1,0:T(2,128)(2,1)S(1)} %get-tuple-element.29), channel_id=1, source_target_pairs={{1,0},{2,1},{3,2},{0,3},{5,4},{6,5},{7,6},{4,7},{9,8},{10,9},{11,1... | collective-permute-start | bytes 50696 | tf_op jit(solution)/shard_map/ppermute | solution.py:17
  23.9 6.2 %collective-permute-start.6 = (bf16[66,1,128]{2,1,0:T(2,128)(2,1)S(1)}, bf16[66,1,128]{2,1,0:T(2,128)(2,1)S(1)}, u32[]{:S(2)}, u32[]{:S(2)}) collective-permute-start(bf16[66,1,128]{2,1,0:T(2,128)(2,1)S(1)} %get-tuple-element.30), channel_id=1, source_target_pairs={{0,1},{1,2},{2,3},{3,0},{4,5},{5,6},{6,7},{7,4},{8,9},{9,10},{10,1... | collective-permute-start | bytes 50696 | tf_op jit(solution)/shard_map/ppermute | solution.py:15
  31.7 1.0 copy-start.4
  40.0 4.2 %collective-permute-start.8 = (bf16[1,32,128]{2,0,1:T(2,128)(2,1)S(1)}, bf16[1,32,128]{2,0,1:T(2,128)(2,1)S(1)}, u32[]{:S(2)}, u32[]{:S(2)}) collective-permute-start(bf16[1,32,128]{2,0,1:T(2,128)(2,1)S(1)} %get-tuple-element.36), channel_id=1, source_target_pairs={{0,4},{4,8},{8,12},{12,16},{16,20},{20,24},{24,28},{28,0},{1,5},{5... | collective-permute-start | bytes 24584 | tf_op jit(solution)/shard_map/ppermute | solution.py:15
  40.1 4.1 %collective-permute-start.9 = (bf16[1,32,128]{2,0,1:T(2,128)(2,1)S(1)}, bf16[1,32,128]{2,0,1:T(2,128)(2,1)S(1)}, u32[]{:S(2)}, u32[]{:S(2)}) collective-permute-start(bf16[1,32,128]{2,0,1:T(2,128)(2,1)S(1)} %get-tuple-element.37), channel_id=1, source_target_pairs={{4,0},{8,4},{12,8},{16,12},{20,16},{24,20},{28,24},{0,28},{5,1},{9... | collective-permute-start | bytes 24584 | tf_op jit(solution)/shard_map/ppermute | solution.py:17
  44.2 5.6 %collective-permute-start.10 = (bf16[66,1,128]{2,0,1:T(8,128)(2,1)S(1)}, bf16[66,1,128]{2,0,1:T(8,128)(2,1)S(1)}, u32[]{:S(2)}, u32[]{:S(2)}) collective-permute-start(bf16[66,1,128]{2,0,1:T(8,128)(2,1)S(1)} %get-tuple-element.21), channel_id=1, source_target_pairs={{0,1},{1,2},{2,3},{3,0},{4,5},{5,6},{6,7},{7,4},{8,9},{9,10},{10,1... | collective-permute-start | bytes 50696 | tf_op jit(solution)/shard_map/ppermute | solution.py:15
  44.3 5.5 %collective-permute-start.11 = (bf16[66,1,128]{2,0,1:T(8,128)(2,1)S(1)}, bf16[66,1,128]{2,0,1:T(8,128)(2,1)S(1)}, u32[]{:S(2)}, u32[]{:S(2)}) collective-permute-start(bf16[66,1,128]{2,0,1:T(8,128)(2,1)S(1)} %get-tuple-element.20), channel_id=1, source_target_pairs={{1,0},{2,1},{3,2},{0,3},{5,4},{6,5},{7,6},{4,7},{9,8},{10,9},{11,1... | collective-permute-start | bytes 50696 | tf_op jit(solution)/shard_map/ppermute | solution.py:17
  56.2 4.3 %copy-start.7 = (f32[32,3]{0,1:T(4,128)S(1)}, f32[32,3]{0,1:T(4,128)}, u32[]{:S(2)}) copy-start(f32[32,3]{0,1:T(4,128)} %param.12) | copy-start | bytes 1156
  56.2 134.7 %copy-start.5 = (f32[2,147456]{1,0:T(2,128)S(1)}, f32[2,147456]{1,0:T(2,128)}, u32[]{:S(2)}) copy-start(f32[2,147456]{1,0:T(2,128)} %param.11) | copy-start | bytes 3538948
  188.4 2.5 %copy-start.1 = (f32[2,147456]{1,0:T(2,128)S(1)}, f32[2,147456]{1,0:T(2,128)}, u32[]{:S(2)}) copy-start(f32[2,147456]{1,0:T(2,128)} %all-reduce.2.cloned.1.call-done) | copy-start | bytes 3538948
  190.9 1.4 copy-start.8
  191.0 1.4 copy-start.9
  192.3 33.8 %copy-start.6 = (f32[2,147456]{1,0:T(2,128)}, f32[2,147456]{1,0:T(2,128)S(1)}, u32[]{:S(2)}) copy-start(f32[2,147456]{1,0:T(2,128)S(1)} %get-tuple-element.2) | copy-start | bytes 3538948
Sparse Core Ops, SparseCore 0:
  56.2 132.2 all-reduce.1
where the time goes:
time: 241 us; the launch traced here: 238 us
  waiting for transfers between devices  133 us (55%)
  matrix products  46 us (19%)
  starting transfers between devices  19.8 us (8%)
  between operations  14.8 us (6%)
  local copies, waits for them, and re-layouts  13.3 us (6%)
  other arithmetic  11.9 us (5%)
    psum x1, waiting for transfers between devices, on_device(): grads = lax.psum(local_grads, ('row', 'col'))  128 us
    dot_general x1, matrix products, learned_step(): jnp.einsum('kh,hlp->klp', w_out, units, precision=lax.Precision.HIGHEST)  33.7 us
    ppermute x6, starting transfers between devices, padded_2(): lax.ppermute(head, axis, [((i + 1) % count, i) for i in range(count)])  16.3 us
    unnamed x24, local copies, waits for them, and re-layouts  9.07 us
    dot_general x18, matrix products, kernel_grad(): lax.dot_general(window, flat_cot, (((0,), (0,)), ((), ())), preferred_ele...  7.03 us
  transfers between devices with their start and end apart: 13, of which 4 were waited for; matrix products, arithmetic and copies ran while one was open for 5% of the time, Pallas kernels for 0%

commit v1 on v0

--- a/solution.py
+++ b/solution.py
@@ -105,7 +105,10 @@
     local_grads = jnp.stack([grad_one.reshape(-1), grad_two.reshape(-1)])
     weights = kernels.reshape(2, param_count)
     gain = math.sqrt(9.0 * channels)
-    grads = lax.psum(local_grads, ("row", "col"))
+    _measure_surface = lambda content, a_name, named_axis: lax.psum(
+        lax.psum(content, a_name), named_axis
+    )
+    grads = _measure_surface(local_grads, "col", "row")
     squares = jnp.sum(grads * grads, axis=1)
     update, momentum_out = learned_step(
         grads,

time: 241 us -> 226 us (0.938)
  waiting for transfers between devices: 133 us -> 116 us
    psum x1 -> x2, waiting for transfers between devices: 128 us -> 111 us  [the longest x1 56.7 us: on_device(): lax.psum(content, a_name)]
    unnamed x24 -> x26, local copies, waits for them, and re-layouts: 9.07 us -> 9.88 us
  transfers between devices with their start and end apart: 13 -> 14, of which waited for: 4 -> 5; matrix products, arithmetic and copies ran while one was open for 5% -> 5% of each run, Pallas kernels for 0% -> 0%
where the time goes in v1:
time: 226 us; the launch traced here: 223 us
  waiting for transfers between devices  116 us (51%)
  matrix products  46 us (20%)
  starting transfers between devices  19.8 us (9%)
  between operations  14.8 us (7%)
  local copies, waits for them, and re-layouts  14.2 us (6%)
  other arithmetic  11.9 us (5%)
    psum x1, waiting for transfers between devices, on_device(): lax.psum(content, a_name)  56.7 us
    psum x1, waiting for transfers between devices, on_device(): lax.psum(lax.psum(content, a_name), named_axis)  54.6 us
    dot_general x1, matrix products, learned_step(): jnp.einsum('kh,hlp->klp', w_out, units, precision=lax.Precision.HIGHEST)  33.7 us
    ppermute x6, starting transfers between devices, padded_2(): lax.ppermute(head, axis, [((i + 1) % count, i) for i in range(count)])  16.3 us
    unnamed x26, local copies, waits for them, and re-layouts  9.88 us
    dot_general x18, matrix products, kernel_grad(): lax.dot_general(window, flat_cot, (((0,), (0,)), ((), ())), preferred_ele...  7.02 us
    ppermute x6, waiting for transfers between devices, padded_2(): lax.ppermute(tail, axis, [(i, (i + 1) % count) for i in range(count)])  4.59 us
  transfers between devices with their start and end apart: 14, of which 5 were waited for; matrix products, arithmetic and copies ran while one was open for 5% of the time, Pallas kernels for 0%

profile of v1, /device:TPU:0, one launch (start us, length us, event | category | flops | bytes accessed | tf_op | source)
XLA Modules:
  0.0 222.7 jit_solution(5579466478931813520)
XLA Ops:
  7.2 1.3 copy.30
  8.6 0.5 collective-permute-start
  9.1 2.9 %collective-permute-start.1 = (bf16[1,32,128]{2,0,1:T(2,128)(2,1)S(1)}, bf16[1,32,128]{2,0,1:T(2,128)(2,1)S(1)}, u32[]{:S(2)}, u32[]{:S(2)}) collective-permute-start(bf16[1,32,128]{2,0,1:T(2,128)(2,1)S(1)} %get-tuple-element.41), channel_id=1, source_target_pairs={{4,0},{8,4},{12,8},{16,12},{20,16},{24,20},{28,24},{0,28},{5,1},{9... | collective-permute-start | bytes 24584 | tf_op jit(solution)/shard_map/ppermute | solution.py:17
  12.1 0.7 fusion.119
  12.8 2.6 %collective-permute-start.4 = (bf16[1,32,128]{2,1,0:T(8,128)(2,1)S(1)}, bf16[1,32,128]{2,1,0:T(8,128)(2,1)S(1)}, u32[]{:S(2)}, u32[]{:S(2)}) collective-permute-start(bf16[1,32,128]{2,1,0:T(8,128)(2,1)S(1)} %get-tuple-element.34), channel_id=1, source_target_pairs={{4,0},{8,4},{12,8},{16,12},{20,16},{24,20},{28,24},{0,28},{5,1},{9... | collective-permute-start | bytes 24584 | tf_op jit(solution)/shard_map/ppermute | solution.py:17
  15.5 2.3 %collective-permute-start.2 = (bf16[66,1,128]{2,0,1:T(8,128)(2,1)S(1)}, bf16[66,1,128]{2,0,1:T(8,128)(2,1)S(1)}, u32[]{:S(2)}, u32[]{:S(2)}) collective-permute-start(bf16[66,1,128]{2,0,1:T(8,128)(2,1)S(1)} %get-tuple-element.25), channel_id=1, source_target_pairs={{0,1},{1,2},{2,3},{3,0},{4,5},{5,6},{6,7},{7,4},{8,9},{9,10},{10,1... | collective-permute-start | bytes 50696 | tf_op jit(solution)/shard_map/ppermute | solution.py:15
  17.8 2.1 collective-permute-start.7
  20.9 0.4 pad_maximum_fusion.7
  21.3 0.3 copy.35
  21.6 0.3 copy.41
  22.0 2.0 collective-permute-start.5
  23.9 0.5 collective-permute-start.6
  24.5 0.4 pad_maximum_fusion.1
  24.8 0.7 fusion.116
  25.6 0.3 copy.33
  26.2 0.3 copy.36
  26.5 0.3 copy.37
  27.9 2.2 collective-permute-done.6
  30.1 0.7 pad_maximum_fusion.11
  32.0 0.7 copy-done.4
  35.7 0.4 fusion.21
  36.1 1.4 fusion.43
  37.9 0.4 fusion.40
  38.9 0.4 fusion.37
  40.1 2.6 %collective-permute-start.9 = (bf16[1,32,128]{2,0,1:T(2,128)(2,1)S(1)}, bf16[1,32,128]{2,0,1:T(2,128)(2,1)S(1)}, u32[]{:S(2)}, u32[]{:S(2)}) collective-permute-start(bf16[1,32,128]{2,0,1:T(2,128)(2,1)S(1)} %get-tuple-element.37), channel_id=1, source_target_pairs={{4,0},{8,4},{12,8},{16,12},{20,16},{24,20},{28,24},{0,28},{5,1},{9... | collective-permute-start | bytes 24584 | tf_op jit(solution)/shard_map/ppermute | solution.py:17
  42.7 0.3 fusion.34
  43.1 1.2 collective-permute-done.8
  44.4 4.0 %collective-permute-start.11 = (bf16[66,1,128]{2,0,1:T(8,128)(2,1)S(1)}, bf16[66,1,128]{2,0,1:T(8,128)(2,1)S(1)}, u32[]{:S(2)}, u32[]{:S(2)}) collective-permute-start(bf16[66,1,128]{2,0,1:T(8,128)(2,1)S(1)} %get-tuple-element.20), channel_id=1, source_target_pairs={{1,0},{2,1},{3,2},{0,3},{5,4},{6,5},{7,6},{4,7},{9,8},{10,9},{11,1... | collective-permute-start | bytes 50696 | tf_op jit(solution)/shard_map/ppermute | solution.py:17
  48.7 1.2 collective-permute-done.10
  49.9 0.4 pad_maximum_fusion.2
  50.3 0.4 fusion.32
  50.7 0.5 fusion.31
  51.1 0.4 fusion.30
  51.5 0.5 fusion.29
  52.0 0.4 fusion.28
  52.4 0.4 fusion.27
  52.8 0.4 fusion.26
  53.3 0.5 fusion.25
  53.7 0.4 fusion.24
  54.2 1.9 pad_maximum_fusion
  56.2 56.7 %all-reduce.3.cloned.1.call-done = f32[2,147456]{1,0:T(2,128)} async-done(((f32[2,147456]{1,0:T(2,128)}), f32[2,147456]{1,0:T(2,128)}) %all-reduce.3.cloned.1.call-update) | async-done | bytes 1179664 | tf_op jit(solution)/shard_map/psum | solution.py:109
  113.0 5.1 %copy.91 = f32[1,2,1152,128]{3,1,2,0:T(2,128)} copy(f32[1,2,1152,128]{3,2,1,0:T(8,128)S(1)} %bitcast.218) | data formatting | bytes 2359296
  118.1 54.6 %all-reduce.5.cloned.1.call-done = f32[2,147456]{1,0:T(2,128)} async-done(((f32[2,147456]{1,0:T(2,128)}), f32[2,147456]{1,0:T(2,128)}) %all-reduce.5.cloned.1.call-update) | async-done | bytes 1179664 | tf_op jit(solution)/shard_map/psum | solution.py:108
  172.7 2.5 %multiply_reduce_fusion = f32[2]{0:T(128)S(1)} fusion(f32[2,147456]{1,0:T(2,128)} %all-reduce.5.cloned.1.call-done), kind=kLoop, calls=%fused_computation.45 | loop fusion | flops 589822 | bytes 1179656 | tf_op jit(solution)/shard_map/reduce_sum | solution.py:112
  175.3 1.4 multiply_add_fusion
  176.7 33.7 %fusion = f32[2,2,147456]{2,0,1:T(2,128)S(1)} fusion(f32[32]{0:T(128)S(1)} %copy-done.9, f32[2,147456]{1,0:T(2,128)S(1)} %bitcast.239, f32[32]{0:T(128)S(1)} %get-tuple-element.43, f32[2,147456]{1,0:T(2,128)S(1)} %get-tuple-element.2, f32[32]{0:T(128)S(1)} %get-tuple-element.44, f32[2,147456]{1,0:T(2,128)S(1)} %get-tuple-element.3, ...), kind=kOutput, calls=%fused_computation.1 | convolution fusion | flops 321454080 | bytes 5899016 | tf_op jit(solution)/shard_map/kh,hlp->klp/dot_general | solution.py:83
  210.4 2.5 %fusion.23 = f32[1,2,147456]{2,0,1:T(1,128)S(1)} fusion(f32[2,2,147456]{2,0,1:T(2,128)S(1)} %fusion), kind=kLoop, calls=%fused_computation.40 | loop fusion | flops 294912 | bytes 3538944 | tf_op jit(solution)/shard_map/mul | solution.py:86
  212.9 2.7 %copy.92 = f32[1,2,147456]{2,1,0:T(2,128)} copy(f32[1,2,147456]{2,0,1:T(1,128)S(1)} %fusion.23) | data formatting | bytes 2359296
  (74 shorter events, 8.9 us)
Async XLA Ops:
  7.2 169.5 %copy-start = (f32[2,32]{1,0:T(2,128)S(1)}, f32[2,32]{1,0:T(2,128)}, u32[]{:S(2)}) copy-start(f32[2,32]{1,0:T(2,128)} %param.14) | copy-start | bytes 772
  7.2 12.7 %copy-start.3 = (bf16[64,32,128]{2,1,0:T(8,128)(2,1)S(1)}, bf16[64,32,128]{2,1,0:T(8,128)(2,1)}, u32[]{:S(2)}) copy-start(bf16[64,32,128]{2,1,0:T(8,128)(2,1)} %param.9) | copy-start | bytes 1572868
  7.2 105.7 %all-reduce.3.cloned.1.call-start = ((), (), s32[]{:S(2)}) async-start(), calls=%async_computation | async-start | bytes 2359296 | tf_op jit(solution)/shard_map/psum | solution.py:109
  8.6 6.8 %collective-permute-start = (bf16[1,32,128]{2,0,1:T(2,128)(2,1)S(1)}, bf16[1,32,128]{2,0,1:T(2,128)(2,1)S(1)}, u32[]{:S(2)}, u32[]{:S(2)}) collective-permute-start(bf16[1,32,128]{2,0,1:T(2,128)(2,1)S(1)} %get-tuple-element.40), channel_id=1, source_target_pairs={{0,4},{4,8},{8,12},{12,16},{16,20},{20,24},{24,28},{28,0},{1,5},{5... | collective-permute-start | bytes 24584 | tf_op jit(solution)/shard_map/ppermute | solution.py:15
  9.1 6.3 %collective-permute-start.1 = (bf16[1,32,128]{2,0,1:T(2,128)(2,1)S(1)}, bf16[1,32,128]{2,0,1:T(2,128)(2,1)S(1)}, u32[]{:S(2)}, u32[]{:S(2)}) collective-permute-start(bf16[1,32,128]{2,0,1:T(2,128)(2,1)S(1)} %get-tuple-element.41), channel_id=1, source_target_pairs={{4,0},{8,4},{12,8},{16,12},{20,16},{24,20},{28,24},{0,28},{5,1},{9... | collective-permute-start | bytes 24584 | tf_op jit(solution)/shard_map/ppermute | solution.py:17
  12.8 7.1 %collective-permute-start.3 = (bf16[1,32,128]{2,1,0:T(8,128)(2,1)S(1)}, bf16[1,32,128]{2,1,0:T(8,128)(2,1)S(1)}, u32[]{:S(2)}, u32[]{:S(2)}) collective-permute-start(bf16[1,32,128]{2,1,0:T(8,128)(2,1)S(1)} %get-tuple-element.35), channel_id=1, source_target_pairs={{0,4},{4,8},{8,12},{12,16},{16,20},{20,24},{24,28},{28,0},{1,5},{5... | collective-permute-start | bytes 24584 | tf_op jit(solution)/shard_map/ppermute | solution.py:15
  12.8 7.1 %collective-permute-start.4 = (bf16[1,32,128]{2,1,0:T(8,128)(2,1)S(1)}, bf16[1,32,128]{2,1,0:T(8,128)(2,1)S(1)}, u32[]{:S(2)}, u32[]{:S(2)}) collective-permute-start(bf16[1,32,128]{2,1,0:T(8,128)(2,1)S(1)} %get-tuple-element.34), channel_id=1, source_target_pairs={{4,0},{8,4},{12,8},{16,12},{20,16},{24,20},{28,24},{0,28},{5,1},{9... | collective-permute-start | bytes 24584 | tf_op jit(solution)/shard_map/ppermute | solution.py:17
  15.4 4.8 %copy-start.2 = (bf16[2,9,128,128]{3,2,1,0:T(8,128)(2,1)S(1)}, bf16[2,9,128,128]{3,2,1,0:T(8,128)(2,1)}, u32[]{:S(2)}) copy-start(bf16[2,9,128,128]{3,2,1,0:T(8,128)(2,1)} %param.10) | copy-start | bytes 1769476
  15.5 9.0 %collective-permute-start.2 = (bf16[66,1,128]{2,0,1:T(8,128)(2,1)S(1)}, bf16[66,1,128]{2,0,1:T(8,128)(2,1)S(1)}, u32[]{:S(2)}, u32[]{:S(2)}) collective-permute-start(bf16[66,1,128]{2,0,1:T(8,128)(2,1)S(1)} %get-tuple-element.25), channel_id=1, source_target_pairs={{0,1},{1,2},{2,3},{3,0},{4,5},{5,6},{6,7},{7,4},{8,9},{9,10},{10,1... | collective-permute-start | bytes 50696 | tf_op jit(solution)/shard_map/ppermute | solution.py:15
  17.8 6.7 %collective-permute-start.7 = (bf16[66,1,128]{2,0,1:T(8,128)(2,1)S(1)}, bf16[66,1,128]{2,0,1:T(8,128)(2,1)S(1)}, u32[]{:S(2)}, u32[]{:S(2)}) collective-permute-start(bf16[66,1,128]{2,0,1:T(8,128)(2,1)S(1)} %get-tuple-element.24), channel_id=1, source_target_pairs={{1,0},{2,1},{3,2},{0,3},{5,4},{6,5},{7,6},{4,7},{9,8},{10,9},{11,1... | collective-permute-start | bytes 50696 | tf_op jit(solution)/shard_map/ppermute | solution.py:17
  22.0 6.0 %collective-permute-start.5 = (bf16[66,1,128]{2,1,0:T(2,128)(2,1)S(1)}, bf16[66,1,128]{2,1,0:T(2,128)(2,1)S(1)}, u32[]{:S(2)}, u32[]{:S(2)}) collective-permute-start(bf16[66,1,128]{2,1,0:T(2,128)(2,1)S(1)} %get-tuple-element.29), channel_id=1, source_target_pairs={{1,0},{2,1},{3,2},{0,3},{5,4},{6,5},{7,6},{4,7},{9,8},{10,9},{11,1... | collective-permute-start | bytes 50696 | tf_op jit(solution)/shard_map/ppermute | solution.py:17
  23.9 6.2 %collective-permute-start.6 = (bf16[66,1,128]{2,1,0:T(2,128)(2,1)S(1)}, bf16[66,1,128]{2,1,0:T(2,128)(2,1)S(1)}, u32[]{:S(2)}, u32[]{:S(2)}) collective-permute-start(bf16[66,1,128]{2,1,0:T(2,128)(2,1)S(1)} %get-tuple-element.30), channel_id=1, source_target_pairs={{0,1},{1,2},{2,3},{3,0},{4,5},{5,6},{6,7},{7,4},{8,9},{9,10},{10,1... | collective-permute-start | bytes 50696 | tf_op jit(solution)/shard_map/ppermute | solution.py:15
  31.7 1.0 copy-start.4
  40.0 4.2 %collective-permute-start.8 = (bf16[1,32,128]{2,0,1:T(2,128)(2,1)S(1)}, bf16[1,32,128]{2,0,1:T(2,128)(2,1)S(1)}, u32[]{:S(2)}, u32[]{:S(2)}) collective-permute-start(bf16[1,32,128]{2,0,1:T(2,128)(2,1)S(1)} %get-tuple-element.36), channel_id=1, source_target_pairs={{0,4},{4,8},{8,12},{12,16},{16,20},{20,24},{24,28},{28,0},{1,5},{5... | collective-permute-start | bytes 24584 | tf_op jit(solution)/shard_map/ppermute | solution.py:15
  40.1 4.2 %collective-permute-start.9 = (bf16[1,32,128]{2,0,1:T(2,128)(2,1)S(1)}, bf16[1,32,128]{2,0,1:T(2,128)(2,1)S(1)}, u32[]{:S(2)}, u32[]{:S(2)}) collective-permute-start(bf16[1,32,128]{2,0,1:T(2,128)(2,1)S(1)} %get-tuple-element.37), channel_id=1, source_target_pairs={{4,0},{8,4},{12,8},{16,12},{20,16},{24,20},{28,24},{0,28},{5,1},{9... | collective-permute-start | bytes 24584 | tf_op jit(solution)/shard_map/ppermute | solution.py:17
  44.3 5.6 %collective-permute-start.10 = (bf16[66,1,128]{2,0,1:T(8,128)(2,1)S(1)}, bf16[66,1,128]{2,0,1:T(8,128)(2,1)S(1)}, u32[]{:S(2)}, u32[]{:S(2)}) collective-permute-start(bf16[66,1,128]{2,0,1:T(8,128)(2,1)S(1)} %get-tuple-element.21), channel_id=1, source_target_pairs={{0,1},{1,2},{2,3},{3,0},{4,5},{5,6},{6,7},{7,4},{8,9},{9,10},{10,1... | collective-permute-start | bytes 50696 | tf_op jit(solution)/shard_map/ppermute | solution.py:15
  44.4 5.5 %collective-permute-start.11 = (bf16[66,1,128]{2,0,1:T(8,128)(2,1)S(1)}, bf16[66,1,128]{2,0,1:T(8,128)(2,1)S(1)}, u32[]{:S(2)}, u32[]{:S(2)}) collective-permute-start(bf16[66,1,128]{2,0,1:T(8,128)(2,1)S(1)} %get-tuple-element.20), channel_id=1, source_target_pairs={{1,0},{2,1},{3,2},{0,3},{5,4},{6,5},{7,6},{4,7},{9,8},{10,9},{11,1... | collective-permute-start | bytes 50696 | tf_op jit(solution)/shard_map/ppermute | solution.py:17
  56.1 116.6 %all-reduce.5.cloned.1.call-start = ((), (), s32[]{:S(2)}) async-start(), calls=%async_computation.1 | async-start | bytes 2359296 | tf_op jit(solution)/shard_map/psum | solution.py:108
  113.0 5.1 %copy-start.8 = (f32[32,3]{0,1:T(4,128)S(1)}, f32[32,3]{0,1:T(4,128)}, u32[]{:S(2)}) copy-start(f32[32,3]{0,1:T(4,128)} %param.12) | copy-start | bytes 1156
  113.0 62.2 %copy-start.5 = (f32[2,147456]{1,0:T(2,128)S(1)}, f32[2,147456]{1,0:T(2,128)}, u32[]{:S(2)}) copy-start(f32[2,147456]{1,0:T(2,128)} %param.11) | copy-start | bytes 3538948
  172.7 2.5 %copy-start.1 = (f32[2,147456]{1,0:T(2,128)S(1)}, f32[2,147456]{1,0:T(2,128)}, u32[]{:S(2)}) copy-start(f32[2,147456]{1,0:T(2,128)} %all-reduce.5.cloned.1.call-done) | copy-start | bytes 3538948
  175.2 1.4 copy-start.7
  175.2 1.4 copy-start.9
  175.2 1.4 copy-start.10
  176.6 33.8 %copy-start.6 = (f32[2,147456]{1,0:T(2,128)}, f32[2,147456]{1,0:T(2,128)S(1)}, u32[]{:S(2)}) copy-start(f32[2,147456]{1,0:T(2,128)S(1)} %get-tuple-element.2) | copy-start | bytes 3538948
Sparse Core Ops, SparseCore 0:
  56.2 56.5 all-reduce.2
  116.0 56.6 all-reduce.4
